TPU v7x, 1024 devices: a whole 4x8x16 slice. The times are simulated.
1024 devices in a mesh: dp: 32 (over z, core), expert: 32 (over y, x).
Axes of the slice: x: 4, y: 8, z: 16, core: 2. Of those that a mesh axis runs over, the one named last changes fastest.
Arguments:
- tokens: bfloat16 [32768, 2048], P(('dp', 'expert')), may hold values from -6 to 6
- routes: int32 [32768, 6], P(('dp', 'expert')), may hold values from 0 to 31, all different within a row; in each aligned block of 32 rows (0 to 31, 32 to 63, ...) at most 7 rows name the same one
- weights_fwd: float32 [32768, 6], P(('dp', 'expert')), may hold values from 0.05 to 0.45
- cotangent: bfloat16 [32768, 2048], P(('dp', 'expert')), may hold values from -6 to 6
- routes_back: int32 [32768, 6], P(('dp', 'expert')), may hold values from 0 to 31, all different within a row; in each aligned block of 32 rows (0 to 31, 32 to 63, ...) at most 7 rows name the same one
- weights_back: float32 [32768, 6], P(('dp', 'expert')), may hold values from 0.05 to 0.45
- saved_gate: bfloat16 [32, 32, 32, 7, 704], P('dp', None, 'expert'), may hold values from -5 to 5
- saved_up: bfloat16 [32, 32, 32, 7, 704], P('dp', None, 'expert'), may hold values from -5 to 5
- w_gate: bfloat16 [32, 2048, 704], P('expert'), may hold values from -0.125 to 0.125
- w_up: bfloat16 [32, 2048, 704], P('expert'), may hold values from -0.125 to 0.125
- w_down: bfloat16 [32, 704, 2048], P('expert'), may hold values from -0.21875 to 0.21875
Outputs:
- mixed: bfloat16 [32768, 2048], P(('dp', 'expert'))
- input_grad: bfloat16 [32768, 2048], P(('dp', 'expert'))
- weight_grad: float32 [32768, 6], P(('dp', 'expert'))
Inputs may be any that keep to these rules, and one draw needn't show every extreme that they name: `routes`: each row names 6 different experts; among the 32 rows of one device no expert is named more than 7 times, and in every draw some expert is named exactly 7 times by one device. `routes_back`: each row names 6 different experts; among the 32 rows of one device no expert is named more than 7 times, and in every draw some expert is named exactly 7 times by one device.
All inputs are finite; a program needn't handle non-finite values.
Results may differ from a plain program's by a relative error of at most 0.0057.
Values may be sent and summed in bfloat16 or wider, within the bound.
A program may use at most 64 MiB of HBM per device.

v0:
```python
import jax
import jax.numpy as jnp
from jax import lax
from jax.sharding import PartitionSpec as P

EXPERTS = 32
CAP = 7


def slot_places(ids):
    count, top = ids.shape
    flat = ids.reshape(-1)
    onehot = (flat[:, None] == jnp.arange(EXPERTS, dtype=jnp.int32)[None, :]).astype(jnp.int32)
    before = jnp.cumsum(onehot, axis=0) - onehot
    slot = jnp.sum(before * onehot, axis=1)
    return (flat * CAP + slot).reshape(count, top)


def dispatch(places, rows, owners):
    count, top = places.shape
    table = places.reshape(-1)[None, :] == jnp.arange(EXPERTS * CAP, dtype=jnp.int32)[:, None]
    table = jnp.sum(table.reshape(EXPERTS * CAP, count, top).astype(jnp.int32), axis=2).astype(
        jnp.bfloat16
    )
    packed = jnp.dot(table, rows, preferred_element_type=jnp.float32).astype(jnp.bfloat16)
    return packed.reshape(owners, EXPERTS // owners, CAP, rows.shape[1])


def combine(flat_out, places, factors):
    picked = flat_out[places].astype(jnp.float32)
    return jnp.sum(factors[:, :, None] * picked, axis=1)


def expert_forward(received, w_gate, w_up, w_down):
    gate = jnp.einsum("secd,edf->secf", received, w_gate, preferred_element_type=jnp.float32)
    up = jnp.einsum("secd,edf->secf", received, w_up, preferred_element_type=jnp.float32)
    hidden = (jax.nn.silu(gate) * up).astype(jnp.bfloat16)
    return jnp.einsum("secf,efd->secd", hidden, w_down, preferred_element_type=jnp.float32).astype(
        jnp.bfloat16
    )


def expert_backward(received, saved_gate, saved_up, w_gate, w_up, w_down):
    act_in = saved_gate.astype(jnp.float32)
    up_in = saved_up.astype(jnp.float32)
    grad_hidden = jnp.einsum("secd,efd->secf", received, w_down, preferred_element_type=jnp.float32)
    sig = jax.nn.sigmoid(act_in)
    silu_in = act_in * sig
    score = jnp.sum(silu_in * up_in * grad_hidden, axis=3)
    grad_gate = (grad_hidden * up_in * sig * (1.0 + act_in * (1.0 - sig))).astype(jnp.bfloat16)
    grad_up = (grad_hidden * silu_in).astype(jnp.bfloat16)
    result = jnp.einsum("secf,edf->secd", grad_gate, w_gate, preferred_element_type=jnp.float32)
    result = result + jnp.einsum(
        "secf,edf->secd", grad_up, w_up, preferred_element_type=jnp.float32
    )
    return (result.astype(jnp.bfloat16), score)


def body(
    tokens,
    routes,
    weights_fwd,
    cotangent,
    routes_back,
    weights_back,
    saved_gate,
    saved_up,
    w_gate,
    w_up,
    w_down,
):
    owners = lax.axis_size("expert")
    places = slot_places(routes)
    places_back = slot_places(routes_back)
    buffer = dispatch(places, tokens, owners)
    grad_buffer = dispatch(places_back, cotangent, owners)
    kept_gate = saved_gate[0]
    kept_up = saved_up[0]
    outputs = expert_forward(
        lax.all_to_all(buffer, "expert", split_axis=0, concat_axis=0, tiled=True),
        w_gate,
        w_up,
        w_down,
    )
    returned = lax.all_to_all(outputs, "expert", split_axis=0, concat_axis=0, tiled=True)
    grad_in = lax.all_to_all(grad_buffer, "expert", split_axis=0, concat_axis=0, tiled=True)
    expert_grad, score = expert_backward(grad_in, kept_gate, kept_up, w_gate, w_up, w_down)
    grad_back, score_back = (
        lax.all_to_all(
            expert_grad.astype(jnp.float32), "expert", split_axis=0, concat_axis=0, tiled=True
        ).astype(expert_grad.dtype),
        lax.all_to_all(score, "expert", split_axis=0, concat_axis=0, tiled=True),
    )
    width = tokens.shape[1]
    mixed = combine(returned.reshape(EXPERTS * CAP, width), places, weights_fwd).astype(
        jnp.bfloat16
    )
    input_grad = combine(grad_back.reshape(EXPERTS * CAP, width), places_back, weights_back).astype(
        jnp.bfloat16
    )
    weight_grad = score_back.reshape(EXPERTS * CAP)[places_back]
    return (mixed, input_grad, weight_grad)


def solution(mesh):
    return jax.shard_map(
        body,
        mesh=mesh,
        in_specs=(
            P(("dp", "expert"), None),
            P(("dp", "expert"), None),
            P(("dp", "expert"), None),
            P(("dp", "expert"), None),
            P(("dp", "expert"), None),
            P(("dp", "expert"), None),
            P("dp", None, "expert", None, None),
            P("dp", None, "expert", None, None),
            P("expert", None, None),
            P("expert", None, None),
            P("expert", None, None),
        ),
        out_specs=(P(("dp", "expert"), None), P(("dp", "expert"), None), P(("dp", "expert"), None)),
        check_vma=False,
    )
```

profile of v0, /device:TPU:66, one launch (start us, length us, event | category | flops | bytes accessed | tf_op | source)
XLA Modules:
  0.0 182.0 jit_solution(13184311542254594468)
XLA Ops:
  0.7 0.9 copy.81
  3.0 2.3 %convolution_convert_fusion = bf16[224,2048]{1,0:T(8,128)(2,1)} fusion(bf16[32,2048]{1,0:T(8,128)(2,1)} %param.14, s32[224,32]{0,1:T(8,128)S(1)} %convert_reduce_fusion.1), kind=kOutput, calls=%fused_computation.18 | convolution fusion | flops 29826048 | bytes 1077248 | tf_op jit(solution)/shard_map/dot_general | solution.py:25
  5.2 2.4 %reshape.218 = bf16[32,1,7,2048]{3,2,0,1:T(8,128)(2,1)} reshape(bf16[224,2048]{1,0:T(8,128)(2,1)} %convolution_convert_fusion) | data formatting | bytes 1835008 | tf_op jit(solution)/shard_map/reshape | solution.py:26
  7.6 10.3 %all-to-all-start.2 = ((bf16[32,1,7,2048]{3,2,1,0:T(8,128)(2,1)}), bf16[32,1,7,2048]{3,2,1,0:T(8,128)(2,1)}, u32[]{:S(2)}, u32[]{:S(2)}) async-start(bf16[32,1,7,2048]{3,2,1,0:T(8,128)(2,1)} %bitcast.163), calls=%async_computation.2 | async-start | bytes 2097152 | tf_op jit(solution)/shard_map/all_to_all | solution.py:86
  19.4 1.4 convolution_convert_fusion.1
  20.8 2.3 %reshape.209 = bf16[32,1,7,2048]{3,2,0,1:T(8,128)(2,1)} reshape(bf16[224,2048]{1,0:T(8,128)(2,1)} %convolution_convert_fusion.1) | data formatting | bytes 1835008 | tf_op jit(solution)/shard_map/reshape | solution.py:26
  23.1 23.0 %all-to-all-done.2 = bf16[32,1,7,2048]{3,2,1,0:T(8,128)(2,1)} async-done(((bf16[32,1,7,2048]{3,2,1,0:T(8,128)(2,1)}), bf16[32,1,7,2048]{3,2,1,0:T(8,128)(2,1)}, u32[]{:S(2)}, u32[]{:S(2)}) %all-to-all-start.2) | async-done | bytes 917536 | tf_op jit(solution)/shard_map/all_to_all | solution.py:86
  46.0 5.6 %all-to-all-start = ((bf16[32,1,7,2048]{3,2,1,0:T(8,128)(2,1)}), bf16[32,1,7,2048]{3,2,1,0:T(8,128)(2,1)}, u32[]{:S(2)}, u32[]{:S(2)}) async-start(bf16[32,1,7,2048]{3,2,1,0:T(8,128)(2,1)} %bitcast.164), calls=%async_computation | async-start | bytes 2097152 | tf_op jit(solution)/shard_map/all_to_all | solution.py:80
  51.7 4.4 %fusion.58 = (f32[32,7]{0,1:T(8,128)S(1)}, f32[32,1,7,704]{3,0,2,1:T(8,128)}) fusion(bf16[1,32,1,7,704]{4,1,3,2,0:T(8,128)(2,1)S(1)} %copy-done.5, bf16[1,32,1,7,704]{4,1,3,2,0:T(8,128)(2,1)} %param.17, bf16[1,704,2048]{2,1,0:T(8,128)(2,1)} %param.21, bf16[32,1,7,2048]{3,2,1,0:T(8,128)(2,1)} %all-to-all-done.2), kind=kOutput, calls=%fused_computation.47 | convolution fusion | flops 647341824 | bytes 5063552 | tf_op jit(solution)/shard_map/secd,efd->secf/dot_general | solution.py:46
  56.7 3.4 %fusion.4 = f32[32,7,2048]{2,0,1:T(8,128)} fusion(bf16[1,2048,704]{1,2,0:T(8,128)(2,1)S(1)} %copy-done, f32[32,1,7,704]{3,0,2,1:T(8,128)} %get-tuple-element.20, bf16[1,32,1,7,704]{4,1,3,2,0:T(8,128)(2,1)} %param.17), kind=kOutput, calls=%fused_computation.7 | convolution fusion | flops 647026688 | bytes 5664768 | tf_op jit(solution)/shard_map/secf,edf->secd/dot_general | solution.py:53
  60.1 18.6 %all-to-all-done = bf16[32,1,7,2048]{3,2,1,0:T(8,128)(2,1)} async-done(((bf16[32,1,7,2048]{3,2,1,0:T(8,128)(2,1)}), bf16[32,1,7,2048]{3,2,1,0:T(8,128)(2,1)}, u32[]{:S(2)}, u32[]{:S(2)}) %all-to-all-start) | async-done | bytes 917536 | tf_op jit(solution)/shard_map/all_to_all | solution.py:80
  78.7 5.6 %all-to-all-start.4 = ((f32[32,1,7]{2,1,0:T(1,128)}), f32[32,1,7]{2,1,0:T(1,128)S(1)}, u32[]{:S(2)}, u32[]{:S(2)}) async-start(f32[32,1,7]{2,1,0:T(1,128)} %copy.89), calls=%async_computation.4 | async-start | bytes 32768 | tf_op jit(solution)/shard_map/all_to_all | solution.py:92
  84.3 3.8 %fusion.27 = bf16[32,1,7,2048]{3,0,2,1:T(8,128)(2,1)S(1)} fusion(f32[32,7,2048]{2,0,1:T(8,128)} %fusion.4, bf16[1,2048,704]{1,2,0:T(8,128)(2,1)} %param.19, f32[32,1,7,704]{3,0,2,1:T(8,128)} %get-tuple-element.20, bf16[1,32,1,7,704]{4,1,3,2,0:T(8,128)(2,1)S(1)} %copy-done.5, bf16[1,32,1,7,704]{4,1,3,2,0:T(8,128)(2,1)} %param.17), kind=kOutput, calls=%fused_computation.22 | convolution fusion | flops 648732672 | bytes 6897664 | tf_op jit(solution)/shard_map/secf,edf->secd/dot_general | solution.py:52
  88.1 2.7 %copy.117 = bf16[32,1,7,2048]{3,1,2,0:T(2,128)(2,1)} copy(bf16[32,1,7,2048]{3,0,2,1:T(8,128)(2,1)S(1)} %fusion.27) | data formatting | bytes 1835008 | tf_op jit(solution)/shard_map/convert_element_type | solution.py:90
  91.3 8.2 %reduce.11 = bf16[32,7,2048]{2,1,0:T(8,128)(2,1)} reduce(bf16[32,7,1,2048]{3,2,1,0:T(2,128)(2,1)} %bitcast.162, bf16[]{:T(256)} %broadcast.147), dimensions={2}, to_apply=%bitcast.161.reduce_sub_computation | reduce | bytes 1835010
  99.5 3.5 %reshape.276 = bf16[32,2,7168]{2,1,0:T(2,128)(2,1)} reshape(bf16[32,7,2048]{2,1,0:T(8,128)(2,1)} %reduce.11) | data formatting | bytes 1835008
  103.0 9.8 %all-to-all-start.3 = ((bf16[32,2,7168]{2,1,0:T(2,128)(2,1)}), bf16[32,2,7168]{2,1,0:T(2,128)(2,1)}, u32[]{:S(2)}, u32[]{:S(2)}) async-start(bf16[32,2,7168]{2,1,0:T(2,128)(2,1)} %reshape.276), calls=%async_computation.3 | async-start | bytes 1835008 | tf_op jit(solution)/shard_map/all_to_all | solution.py:89
  112.8 4.4 %fusion.30 = f32[32,1,7,704]{3,0,2,1:T(8,128)} fusion(bf16[1,2048,704]{1,2,0:T(8,128)(2,1)} %param.19, bf16[32,1,7,2048]{3,2,1,0:T(8,128)(2,1)} %all-to-all-done), kind=kOutput, calls=%fused_computation.26 | convolution fusion | flops 645922816 | bytes 4431872 | tf_op jit(solution)/shard_map/secd,edf->secf/dot_general | solution.py:35
  117.2 5.9 %fusion.21 = bf16[32,1,7,2048]{3,0,2,1:T(8,128)(2,1)} fusion(bf16[1,704,2048]{2,1,0:T(8,128)(2,1)} %param.21, bf16[1,2048,704]{1,2,0:T(8,128)(2,1)S(1)} %copy-done, bf16[32,1,7,2048]{3,2,1,0:T(8,128)(2,1)} %all-to-all-done, f32[32,1,7,704]{3,0,2,1:T(8,128)} %fusion.30), kind=kOutput, calls=%fused_computation.20 | convolution fusion | flops 1293250560 | bytes 8232960 | tf_op jit(solution)/shard_map/secf,efd->secd/dot_general | solution.py:38
  123.1 2.7 %copy.79 = bf16[32,1,7,2048]{3,2,1,0:T(8,128)(2,1)} copy(bf16[32,1,7,2048]{3,0,2,1:T(8,128)(2,1)} %fusion.21) | data formatting | bytes 1835008 | tf_op jit(solution)/shard_map/convert_element_type | solution.py:38
  125.8 10.3 %all-to-all-done.3 = bf16[32,2,7168]{2,1,0:T(2,128)(2,1)} async-done(((bf16[32,2,7168]{2,1,0:T(2,128)(2,1)}), bf16[32,2,7168]{2,1,0:T(2,128)(2,1)}, u32[]{:S(2)}, u32[]{:S(2)}) %all-to-all-start.3) | async-done | bytes 917536 | tf_op jit(solution)/shard_map/all_to_all | solution.py:89
  136.1 5.6 %all-to-all-start.1 = ((bf16[32,1,7,2048]{3,2,1,0:T(8,128)(2,1)}), bf16[32,1,7,2048]{3,2,1,0:T(8,128)(2,1)}, u32[]{:S(2)}, u32[]{:S(2)}) async-start(bf16[32,1,7,2048]{3,2,1,0:T(8,128)(2,1)} %copy.79), calls=%async_computation.1 | async-start | bytes 2097152 | tf_op jit(solution)/shard_map/all_to_all | solution.py:85
  143.5 1.6 gather_fusion.2
  145.9 6.1 %reshape.277 = bf16[32,7,1,2048]{3,2,1,0:T(2,128)(2,1)} reshape(bf16[32,2,7168]{2,1,0:T(2,128)(2,1)} %all-to-all-done.3) | data formatting | bytes 1835008
  152.0 7.8 %convert_reduce_fusion = bf16[32,7,2048]{2,1,0:T(8,128)(2,1)} fusion(bf16[32,7,1,2048]{3,2,1,0:T(2,128)(2,1)} %reshape.277), kind=kLoop, calls=%fused_computation.25 | loop fusion | bytes 1835008 | tf_op jit(solution)/shard_map/convert_element_type | solution.py:91
  159.8 2.3 %reshape.222 = bf16[224,2048]{1,0:T(8,128)(2,1)} reshape(bf16[32,7,2048]{2,1,0:T(8,128)(2,1)} %convert_reduce_fusion) | data formatting | bytes 1835008 | tf_op jit(solution)/shard_map/reshape | solution.py:98
  162.1 4.1 %gather_fusion.1 = bf16[192,2048]{1,0:T(8,128)(2,1)} fusion(bf16[224,2048]{1,0:T(8,128)(2,1)} %reshape.222, s32[1024]{0:T(1024)S(1)} %pad_clamp_fusion), kind=kCustom, calls=%fused_computation.1 | custom fusion | bytes 1573632 | tf_op jit(solution)/shard_map/gather | solution.py:30
  166.2 2.5 %reshape.260 = f32[32,6,2048]{2,1,0:T(8,128)} reshape(bf16[192,2048]{1,0:T(8,128)(2,1)} %gather_fusion.1) | data formatting | bytes 2359296 | tf_op jit(solution)/shard_map/convert_element_type | solution.py:30
  168.7 2.3 %reshape.215 = bf16[224,2048]{1,0:T(8,128)(2,1)} reshape(bf16[32,1,7,2048]{3,2,1,0:T(8,128)(2,1)} %all-to-all-done.1) | data formatting | bytes 1835008 | tf_op jit(solution)/shard_map/reshape | solution.py:95
  171.0 4.1 %gather_fusion = bf16[192,2048]{1,0:T(8,128)(2,1)} fusion(bf16[224,2048]{1,0:T(8,128)(2,1)} %reshape.215, s32[1024]{0:T(1024)S(1)} %pad_clamp_fusion.1), kind=kCustom, calls=%fused_computation | custom fusion | bytes 1573632 | tf_op jit(solution)/shard_map/gather | solution.py:30
  175.1 2.5 %reshape.259 = f32[32,6,2048]{2,1,0:T(8,128)} reshape(bf16[192,2048]{1,0:T(8,128)(2,1)} %gather_fusion) | data formatting | bytes 2359296 | tf_op jit(solution)/shard_map/convert_element_type | solution.py:30
  177.5 4.5 %multiply_reduce_fusion = (bf16[32,2048]{1,0:T(8,128)(2,1)}, bf16[32,2048]{1,0:T(8,128)(2,1)}) fusion(f32[32,6,2048]{2,1,0:T(8,128)} %reshape.260, f32[32,6]{1,0:T(8,128)S(1)} %copy.80, f32[32,6,2048]{2,1,0:T(8,128)} %reshape.259, f32[32,6]{1,0:T(8,128)S(1)} %copy.71), kind=kLoop, calls=%fused_computation.23 | loop fusion | flops 1441792 | bytes 3409408 | tf_op jit(solution)/shard_map/reduce_sum | solution.py:31
  (54 shorter events, 6.5 us)
Async XLA Ops:
  0.6 56.1 %copy-start = (bf16[1,2048,704]{1,2,0:T(8,128)(2,1)S(1)}, bf16[1,2048,704]{1,2,0:T(8,128)(2,1)}, u32[]{:S(2)}) copy-start(bf16[1,2048,704]{1,2,0:T(8,128)(2,1)} %param.20) | copy-start | bytes 8650756
  0.6 17.3 %copy-start.2 = (s32[32,6]{0,1:T(8,128)S(1)}, s32[32,6]{0,1:T(8,128)}, u32[]{:S(2)}) copy-start(s32[32,6]{0,1:T(8,128)} %param.12) | copy-start | bytes 2308
  2.6 16.8 %copy-start.1 = (bf16[32,2048]{1,0:T(8,128)(2,1)S(1)}, bf16[32,2048]{1,0:T(8,128)(2,1)}, u32[]{:S(2)}) copy-start(bf16[32,2048]{1,0:T(8,128)(2,1)} %param.11) | copy-start | bytes 393220
  7.6 38.4 %all-to-all-start.2 = ((bf16[32,1,7,2048]{3,2,1,0:T(8,128)(2,1)}), bf16[32,1,7,2048]{3,2,1,0:T(8,128)(2,1)}, u32[]{:S(2)}, u32[]{:S(2)}) async-start(bf16[32,1,7,2048]{3,2,1,0:T(8,128)(2,1)} %bitcast.163), calls=%async_computation.2 | async-start | bytes 2097152 | tf_op jit(solution)/shard_map/all_to_all | solution.py:86
  17.9 33.7 %copy-start.5 = (bf16[1,32,1,7,704]{4,1,3,2,0:T(8,128)(2,1)S(1)}, bf16[1,32,1,7,704]{4,1,3,2,0:T(8,128)(2,1)}, u32[]{:S(2)}) copy-start(bf16[1,32,1,7,704]{4,1,3,2,0:T(8,128)(2,1)} %param.18) | copy-start | bytes 946180
  46.0 32.7 %all-to-all-start = ((bf16[32,1,7,2048]{3,2,1,0:T(8,128)(2,1)}), bf16[32,1,7,2048]{3,2,1,0:T(8,128)(2,1)}, u32[]{:S(2)}, u32[]{:S(2)}) async-start(bf16[32,1,7,2048]{3,2,1,0:T(8,128)(2,1)} %bitcast.164), calls=%async_computation | async-start | bytes 2097152 | tf_op jit(solution)/shard_map/all_to_all | solution.py:80
  78.7 24.3 %all-to-all-start.4 = ((f32[32,1,7]{2,1,0:T(1,128)}), f32[32,1,7]{2,1,0:T(1,128)S(1)}, u32[]{:S(2)}, u32[]{:S(2)}) async-start(f32[32,1,7]{2,1,0:T(1,128)} %copy.89), calls=%async_computation.4 | async-start | bytes 32768 | tf_op jit(solution)/shard_map/all_to_all | solution.py:92
  103.0 33.1 %all-to-all-start.3 = ((bf16[32,2,7168]{2,1,0:T(2,128)(2,1)}), bf16[32,2,7168]{2,1,0:T(2,128)(2,1)}, u32[]{:S(2)}, u32[]{:S(2)}) async-start(bf16[32,2,7168]{2,1,0:T(2,128)(2,1)} %reshape.276), calls=%async_computation.3 | async-start | bytes 1835008 | tf_op jit(solution)/shard_map/all_to_all | solution.py:89
  123.1 18.9 %copy-start.3 = (f32[32,6]{0,1:T(8,128)S(1)}, f32[32,6]{0,1:T(8,128)}, u32[]{:S(2)}) copy-start(f32[32,6]{0,1:T(8,128)} %param.13) | copy-start | bytes 2308
  123.1 19.0 %copy-start.4 = (f32[32,6]{0,1:T(8,128)S(1)}, f32[32,6]{0,1:T(8,128)}, u32[]{:S(2)}) copy-start(f32[32,6]{0,1:T(8,128)} %param.16) | copy-start | bytes 2308
  136.1 32.5 %all-to-all-start.1 = ((bf16[32,1,7,2048]{3,2,1,0:T(8,128)(2,1)}), bf16[32,1,7,2048]{3,2,1,0:T(8,128)(2,1)}, u32[]{:S(2)}, u32[]{:S(2)}) async-start(bf16[32,1,7,2048]{3,2,1,0:T(8,128)(2,1)} %copy.79), calls=%async_computation.1 | async-start | bytes 2097152 | tf_op jit(solution)/shard_map/all_to_all | solution.py:85
where the time goes:
time: 183 us; the launch traced here: 182 us
  waiting for transfers between devices  51.9 us (28%)
  local copies, waits for them, and re-layouts  51.7 us (28%)
  starting transfers between devices  37 us (20%)
  matrix products  25.4 us (14%)
  other arithmetic  15.1 us (8%)
    all_to_all x1, waiting for transfers between devices, body(): lax.all_to_all(grad_buffer, 'expert', split_axis=0, concat_axis=0, tiled=...  23 us
    all_to_all x1, waiting for transfers between devices, body(): lax.all_to_all(buffer, 'expert', split_axis=0, concat_axis=0, tiled=True)  18.6 us
    unnamed x20, local copies, waits for them, and re-layouts  12 us
    all_to_all x1, waiting for transfers between devices, body(): lax.all_to_all(expert_grad.astype(jnp.float32), 'expert', split_axis=0, c...  10.3 us
    all_to_all x1, starting transfers between devices, body(): lax.all_to_all(grad_buffer, 'expert', split_axis=0, concat_axis=0, tiled=...  10.3 us
    all_to_all x1, starting transfers between devices, body(): lax.all_to_all(expert_grad.astype(jnp.float32), 'expert', split_axis=0, c...  9.85 us
    unnamed x1, other arithmetic  8.22 us
    gather x2, local copies, waits for them, and re-layouts, combine(): picked = flat_out[places].astype(jnp.float32)  8.16 us
  transfers between devices with their start and end apart: 5, of which 3 were waited for; matrix products, arithmetic and copies ran while one was open for 40% of the time, Pallas kernels for 0%

commit v1 on v0

v1 whole, which is shorter than its diff:
```python
import jax
import jax.numpy as jnp
from jax import lax
from jax.experimental import pallas as pl
from jax.experimental.pallas import tpu as pltpu
from jax.sharding import PartitionSpec as P

NX, NY = 4, 8
TOPK = 6
CAP = 7
TOK = 32
NC = 4
PAD = 64
ROWS = CAP * NY
SLOTS = NX * PAD
F32, BF16 = jnp.float32, jnp.bfloat16
DOWN, UP = 0, 1


def nn(a, b):
    return jnp.dot(a, b, preferred_element_type=F32)


def nt(a, b):
    return lax.dot_general(a, b, (((1,), (1,)), ((), ())), preferred_element_type=F32)


def iota(shape, axis):
    return lax.broadcasted_iota(jnp.int32, shape, axis)


def wrap(v, n):
    return jnp.where(v >= n, v - n, v)


def halves(v):
    top = v.astype(BF16)
    return top, (v - top.astype(F32)).astype(BF16)


def hops(c, way):
    return 4 if c % 2 == way else 3


def kernel(
    tok_hbm, cot_hbm, meta_ref, sg_hbm, su_hbm, wg_hbm, wu_hbm, wd_hbm,
    mixed_hbm, grad_hbm, wgrad_ref,
    wg, wu, wd, sg, su, G, XS, X, OUT, OR, PS, R, SB, OB, MS, MR, SCS, SCR, SYS, SYR,
    S, CH, CL, MT, acc_a, acc_b, co_g, co_u, co_s,
    ag_s, ag_r, xd_s, xd_r, xr_s, xr_r, rs_s, rs_r, mt_s, mt_r, sc_s, sc_r, sy_s, sy_r, ld, own, outs,
):
    me = lax.axis_index("expert")
    y, x = lax.div(me, NX), lax.rem(me, NX)
    depth = tok_hbm.shape[1]
    W = depth // NC

    def at_y(o):
        return {"expert": lax.rem(y + o, NY) * NX + x}

    def at_x(p):
        return {"expert": y * NX + lax.rem(x + p, NX)}

    def cols(c):
        return pl.ds(c * W, W)

    ins = (tok_hbm, cot_hbm)
    results = (mixed_hbm, grad_hbm)
    remote = pltpu.make_async_remote_copy

    def gather_hop(m, c, way, h):
        a, b = (h, h + 1) if way == DOWN else ((NY - h) % NY, NY - 1 - h)
        src = ins[m].at[:, cols(c)] if h == 0 else G.at[m, c, a]
        return remote(src, G.at[m, c, b], ag_s.at[m, c, way, h], ag_r.at[m, c, way, h],
                      device_id=at_y(NY - 1 if way == DOWN else 1))

    def to_expert(m, c, p):
        q = NX - p
        return remote(XS.at[m, c, p - 1, pl.ds(0, ROWS)], X.at[m, c, q, pl.ds(0, ROWS)],
                      xd_s.at[m, c, p - 1], xd_r.at[m, c, q - 1], device_id=at_x(p))

    def from_expert(m, c, q):
        p = NX - q
        return remote(OUT.at[m, c, q - 1, pl.ds(0, ROWS)], OR.at[m, c, p, pl.ds(0, ROWS)],
                      xr_s.at[m, c, q - 1], xr_r.at[m, c, p - 1], device_id=at_x(q))

    def sum_hop(m, c, way, k):
        return remote(SB.at[m, c, way, k - 1], R.at[m, c, way, k - 1], rs_s.at[m, c, way, k - 1],
                      rs_r.at[m, c, way, k - 1], device_id=at_y(NY - 1 if way == DOWN else 1))

    def meta_to(o):
        return remote(MS.at[o], MR.at[NY - o], mt_s.at[o - 1], mt_r.at[NY - o - 1], device_id=at_y(o))

    def score_to(q):
        return remote(SCS, SCR.at[NX - q - 1], sc_s.at[q - 1], sc_r.at[NX - q - 1], device_id=at_x(q))

    def score_back(o):
        return remote(SYS.at[o], SYR.at[NY - o], sy_s.at[o - 1], sy_r.at[NY - o - 1], device_id=at_y(o))

    def own_rows(m, c):
        return pltpu.make_async_copy(ins[m].at[:, cols(c)], G.at[m, c, 0], own.at[m, c])

    def result(m, c):
        return pltpu.make_async_copy(OB.at[m, c], results[m].at[:, cols(c)], outs.at[m, c])

    barrier = pltpu.get_barrier_semaphore()
    for o in range(1, NY):
        pl.semaphore_signal(barrier, inc=1, device_id=at_y(o))
    for p in range(1, NX):
        pl.semaphore_signal(barrier, inc=1, device_id=at_x(p))
    loads = [
        pltpu.make_async_copy(a, b, ld.at[i])
        for i, (a, b) in enumerate(((wg_hbm, wg), (wu_hbm, wu), (wd_hbm, wd), (sg_hbm, sg), (su_hbm, su)))
    ]
    for m in range(2):
        for c in range(NC):
            own_rows(m, c).start()
    for load in loads:
        load.start()

    lane = iota((NY, 128), 1)
    named = (wrap(y + iota((NY, 128), 0), NY) * NX + wrap(x + lane // TOK, NX)).astype(F32)
    before = (iota((128, 128), 0) // TOK == iota((128, 128), 1) // TOK) & (iota((128, 128), 0) < iota((128, 128), 1))
    before = before.astype(F32).astype(BF16)
    table = []
    for m in range(2):
        has, weight = jnp.zeros((NY, 128), F32), jnp.zeros((NY, 128), F32)
        for k in range(TOPK):
            hit = named == meta_ref[m, 0, k:k + 1, :]
            has = has + jnp.where(hit, 1.0, 0.0)
            weight = weight + jnp.where(hit, meta_ref[m, 1, k:k + 1, :], 0.0)
        slot = nn(has.astype(BF16), before)
        table += [jnp.where(has > 0, slot, -1.0), weight]
    for o in range(NY):
        for i, rows in enumerate(table):
            MS[o, i:i + 1, :] = rows[o:o + 1, :]
        MS[o, 4:8, :] = jnp.zeros((4, 128), F32)
    MR[0] = MS[0]

    for m in range(2):
        for c in range(NC):
            for p in range(1, NX):
                X[m, c, p, ROWS:PAD, :] = jnp.zeros((PAD - ROWS, W), BF16)
                OR[m, c, p, ROWS:PAD, :] = jnp.zeros((PAD - ROWS, W), BF16)

    pl.semaphore_wait(barrier, NY - 1 + NX - 1)

    def start_own(m):
        for c in range(NC):
            for way in (DOWN, UP):
                gather_hop(m, c, way, 0).start()

    def pass_on(m, h):
        for c in range(NC):
            for way in (DOWN, UP):
                if h < hops(c, way):
                    gather_hop(m, c, way, h - 1).wait_recv()
                    gather_hop(m, c, way, h).start()

    start_own(0)
    for o in range(1, NY):
        meta_to(o).start()

    loads[3].wait()
    loads[4].wait()
    r, cj = iota((SLOTS, CAP * TOK), 0), iota((SLOTS, CAP * TOK), 1)
    source = wrap(y + r % NY, NY) * NX + wrap(x + r // PAD, NX)
    order = ((r % PAD) // NY == cj // 32) & (source == cj % 32)
    order = order.astype(F32).astype(BF16)
    ff = wd_hbm.shape[0]
    a = nn(order, sg[...].reshape(CAP * 32, ff))
    u = nn(order, su[...].reshape(CAP * 32, ff))
    sig = 1.0 / (1.0 + jnp.exp(-a))
    act = a * sig
    co_g[...] = u * sig * (1.0 + a * (1.0 - sig))
    co_u[...] = act
    co_s[...] = act * u

    pass_on(0, 1)
    pass_on(0, 2)
    start_own(1)
    pass_on(0, 3)

    for o in range(1, NY):
        meta_to(o).wait_recv()
    r128, l128 = iota((SLOTS, 128), 0), iota((SLOTS, 128), 1)
    place = l128 // TOK == r128 // PAD
    fold = (r128 % TOK == l128 % TOK).astype(F32).astype(BF16)
    block = iota((SLOTS, SLOTS), 0) % NY == iota((SLOTS, SLOTS), 1) // TOK
    back = iota((SLOTS, SLOTS), 1) % NY == iota((SLOTS, SLOTS), 0) // TOK
    for m in range(2):
        slots = jnp.concatenate([MR[o, 2 * m:2 * m + 1, :] for o in range(NY)], axis=0)
        weights = jnp.concatenate([MR[o, 2 * m + 1:2 * m + 2, :] for o in range(NY)], axis=0)
        slots = jnp.broadcast_to(slots[None], (SLOTS // NY, NY, 128)).reshape(SLOTS, 128)
        weights = jnp.broadcast_to(weights[None], (SLOTS // NY, NY, 128)).reshape(SLOTS, 128)
        hit = (slots == ((r128 % PAD) // NY).astype(F32)) & place
        match = jnp.where(hit, 1.0, 0.0).astype(BF16)
        top, rest = halves(jnp.where(hit, weights, 0.0))
        S[m] = jnp.where(block, nt(match, fold), 0.0).astype(BF16)
        CH[m] = jnp.where(back, nt(fold, top), 0.0).astype(BF16)
        CL[m] = jnp.where(back, nt(fold, rest), 0.0).astype(BF16)
        if m == 1:
            MT[...] = match

    def send_slots(m):
        for c in range(NC):
            own_rows(m, c).wait()
            for way in (DOWN, UP):
                gather_hop(m, c, way, hops(c, way) - 1).wait_recv()
            rows = nn(S[m], G[m, c].reshape(NY * TOK, W)).astype(BF16).reshape(NX, PAD, W)
            for p in range(1, NX):
                XS[m, c, p - 1] = rows[p]
            for p in (2, 1, 3):
                to_expert(m, c, p).start()
            X[m, c, 0] = rows[0]

    def arrived(m, c):
        for p in range(1, NX):
            to_expert(m, c, p).wait_recv()
        return X[m, c].reshape(SLOTS, W)

    def give_back(m, c, value):
        value = value.astype(BF16).reshape(NX, PAD, W)
        for q in range(1, NX):
            OUT[m, c, q - 1] = value[q]
        for q in (2, 1, 3):
            from_expert(m, c, q).start()
        OR[m, c, 0] = value[0]

    send_slots(0)
    pass_on(1, 1)
    pass_on(1, 2)
    pass_on(1, 3)
    send_slots(1)

    for load in loads[:3]:
        load.wait()
    for c in range(NC):
        rows = arrived(0, c)
        g, v = nt(rows, wg[:, cols(c)]), nt(rows, wu[:, cols(c)])
        acc_a[...] = g if c == 0 else acc_a[...] + g
        acc_b[...] = v if c == 0 else acc_b[...] + v
    g = acc_a[...]
    hidden = (g / (1.0 + jnp.exp(-g)) * acc_b[...]).astype(BF16)
    for c in range(NC):
        give_back(0, c, nn(hidden, wd[:, cols(c)]))

    for c in range(NC):
        part = nt(arrived(1, c), wd[:, cols(c)])
        acc_a[...] = part if c == 0 else acc_a[...] + part
    gh = acc_a[...]
    gg, gu = (gh * co_g[...]).astype(BF16), (gh * co_u[...]).astype(BF16)
    top, rest = halves(gh * co_s[...])
    for c in range(NC):
        give_back(1, c, nn(gg, wg[:, cols(c)]) + nn(gu, wu[:, cols(c)]))
    ones = jnp.ones((NY, ff), BF16)
    score = nt(ones, top) + nt(ones, rest)
    SCS[...] = score
    for q in range(1, NX):
        score_to(q).start()

    def send_sum(m, c, way, k):
        o = NY - k if way == DOWN else k
        value = PS[m, c, o]
        if k < hops(c, way):
            sum_hop(m, c, way, k + 1).wait_recv()
            value = value + R[m, c, way, k].astype(F32)
        SB[m, c, way, k - 1] = value.astype(BF16)
        sum_hop(m, c, way, k).start()

    def stage(m, c, s):
        if s == 0:
            for p in range(1, NX):
                from_expert(m, c, NX - p).wait_recv()
            rows = OR[m, c].reshape(SLOTS, W)
            PS[m, c] = (nn(CH[m], rows) + nn(CL[m], rows)).reshape(NY, TOK, W)
        for way in (DOWN, UP):
            if hops(c, way) > s:
                send_sum(m, c, way, hops(c, way) - s)
        if s == 4:
            for way in (DOWN, UP):
                sum_hop(m, c, way, 1).wait_recv()
            OB[m, c] = (PS[m, c, 0] + R[m, c, DOWN, 0].astype(F32) + R[m, c, UP, 0].astype(F32)).astype(BF16)
            result(m, c).start()

    def scores_on():
        mine = iota((NY, PAD), 1) % NY == iota((NY, PAD), 0)
        total = jnp.zeros((NY, 128), F32)
        for p in range(NX):
            if p:
                score_to(NX - p).wait_recv()
            q = (NX - p) % NX
            row = SCS[:, q * PAD:(q + 1) * PAD] if p == 0 else SCR[p - 1, :, q * PAD:(q + 1) * PAD]
            rest = jnp.where(mine, row, 0.0)
            for _ in range(3):
                top, rest2 = rest.astype(BF16), rest - rest.astype(BF16).astype(F32)
                total = total + nn(top, MT[p * PAD:(p + 1) * PAD, :])
                rest = rest2
        for o in range(NY):
            SYS[o] = jnp.broadcast_to(total[o:o + 1, :], (8, 128))
        for o in range(1, NY):
            score_back(o).start()
        SYR[0] = SYS[0]

    def scores_home():
        for o in range(1, NY):
            score_back(o).wait_recv()
        rows = jnp.concatenate([SYR[o, 0:1, :] for o in range(NY)], axis=0)
        for k in range(8):
            v = jnp.sum(jnp.where(named == meta_ref[1, 0, k:k + 1, :], rows, 0.0), axis=0, keepdims=True)
            v = jnp.broadcast_to(v, (8, 128))
            v = v + pltpu.roll(v, 64, 1)
            v = v + pltpu.roll(v, 32, 1)
            wgrad_ref[k:k + 1, :] = v[0:1, :]

    items = [(m, c) for m in range(2) for c in range(NC)]
    for wave in range(len(items) + 4):
        for s in range(4, -1, -1):
            if 0 <= wave - s < len(items):
                stage(*items[wave - s], s)
        if wave == NC:
            scores_on()
        if wave == NC + 4:
            scores_home()

    for m, c in items:
        for way in (DOWN, UP):
            for h in range(hops(c, way)):
                gather_hop(m, c, way, h).wait_send()
                sum_hop(m, c, way, h + 1).wait_send()
        for p in range(1, NX):
            to_expert(m, c, p).wait_send()
            from_expert(m, c, p).wait_send()
    for o in range(1, NY):
        meta_to(o).wait_send()
        score_back(o).wait_send()
    for q in range(1, NX):
        score_to(q).wait_send()
    for m, c in items:
        result(m, c).wait()


def window(tokens, cotangent, meta, saved_gate, saved_up, w_gate, w_up, w_down):
    depth, ff = tokens.shape[1], w_down.shape[0]
    W = depth // NC
    whole = pl.BlockSpec(memory_space=pl.ANY)
    vmem = pl.BlockSpec(memory_space=pltpu.VMEM)
    dma = pltpu.SemaphoreType.DMA
    return pl.pallas_call(
        kernel,
        name="window",
        out_shape=(
            jax.ShapeDtypeStruct((TOK, depth), BF16),
            jax.ShapeDtypeStruct((TOK, depth), BF16),
            jax.ShapeDtypeStruct((8, 128), F32),
        ),
        in_specs=[whole, whole, vmem, whole, whole, whole, whole, whole],
        out_specs=(whole, whole, vmem),
        scratch_shapes=[
            pltpu.VMEM((ff, depth), BF16),
            pltpu.VMEM((ff, depth), BF16),
            pltpu.VMEM((ff, depth), BF16),
            pltpu.VMEM((CAP, 32, ff), BF16),
            pltpu.VMEM((CAP, 32, ff), BF16),
            pltpu.VMEM((2, NC, NY, TOK, W), BF16),
            pltpu.VMEM((2, NC, NX - 1, PAD, W), BF16),
            pltpu.VMEM((2, NC, NX, PAD, W), BF16),
            pltpu.VMEM((2, NC, NX - 1, PAD, W), BF16),
            pltpu.VMEM((2, NC, NX, PAD, W), BF16),
            pltpu.VMEM((2, NC, NY, TOK, W), F32),
            pltpu.VMEM((2, NC, 2, 4, TOK, W), BF16),
            pltpu.VMEM((2, NC, 2, 4, TOK, W), BF16),
            pltpu.VMEM((2, NC, TOK, W), BF16),
            pltpu.VMEM((NY, 8, 128), F32),
            pltpu.VMEM((NY, 8, 128), F32),
            pltpu.VMEM((8, SLOTS), F32),
            pltpu.VMEM((NX - 1, 8, SLOTS), F32),
            pltpu.VMEM((NY, 8, 128), F32),
            pltpu.VMEM((NY, 8, 128), F32),
            pltpu.VMEM((2, SLOTS, SLOTS), BF16),
            pltpu.VMEM((2, SLOTS, SLOTS), BF16),
            pltpu.VMEM((2, SLOTS, SLOTS), BF16),
            pltpu.VMEM((SLOTS, 128), BF16),
            pltpu.VMEM((SLOTS, ff), F32),
            pltpu.VMEM((SLOTS, ff), F32),
            pltpu.VMEM((SLOTS, ff), F32),
            pltpu.VMEM((SLOTS, ff), F32),
            pltpu.VMEM((SLOTS, ff), F32),
            dma((2, NC, 2, 4)), dma((2, NC, 2, 4)),
            dma((2, NC, 3)), dma((2, NC, 3)),
            dma((2, NC, 3)), dma((2, NC, 3)),
            dma((2, NC, 2, 4)), dma((2, NC, 2, 4)),
            dma((7,)), dma((7,)), dma((3,)), dma((3,)), dma((7,)), dma((7,)),
            dma((5,)), dma((2, NC)), dma((2, NC)),
        ],
        compiler_params=pltpu.CompilerParams(
            collective_id=0, has_side_effects=True, vmem_limit_bytes=60 * 1024 * 1024
        ),
    )(tokens, cotangent, meta, saved_gate, saved_up, w_gate, w_up, w_down)


def lanes(routes, weights):
    ids = jnp.pad(routes.T.astype(F32), ((0, 8 - TOPK), (0, 0)), constant_values=-1.0)
    factors = jnp.pad(weights.T, ((0, 8 - TOPK), (0, 0)))
    return jnp.tile(jnp.stack([ids, factors]), (1, 1, 128 // TOK))


def body(
    tokens, routes, weights_fwd, cotangent, routes_back, weights_back, saved_gate, saved_up, w_gate, w_up, w_down
):
    meta = jnp.stack([lanes(routes, weights_fwd), lanes(routes_back, weights_back)])
    mixed, input_grad, wgrad = window(
        tokens, cotangent, meta,
        saved_gate[0, :, 0].transpose(1, 0, 2), saved_up[0, :, 0].transpose(1, 0, 2),
        w_gate[0].T, w_up[0].T, w_down[0],
    )
    return mixed, input_grad, wgrad[:TOPK, :TOK].T


def solution(mesh):
    rows = P(("dp", "expert"), None)
    saved = P("dp", None, "expert", None, None)
    weight = P("expert", None, None)
    return jax.shard_map(
        body,
        mesh=mesh,
        in_specs=(rows,) * 6 + (saved, saved, weight, weight, weight),
        out_specs=(rows, rows, rows),
        check_vma=False,
    )
```

time: 183 us -> 112 us (0.61)
  the two profiles are of different devices: /device:TPU:66 before, /device:TPU:16 now
where the time goes in v1:
time: 112 us
  Pallas kernels  103 us (92%)
  local copies, waits for them, and re-layouts  5.97 us (5%)
  other arithmetic  2 us (2%)
    pallas_call x1, Pallas kernels, window(): pl.pallas_call(kernel, name='window', out_shape=(jax.ShapeDtypeStruct((TO...  103 us
    unnamed x2, local copies, waits for them, and re-layouts  3.13 us

profile of v1, /device:TPU:16, one launch (start us, length us, event | category | flops | bytes accessed | tf_op | source)
XLA Modules:
  0.0 111.6 jit_solution(11158888744193022785)
XLA Ops:
  0.6 0.7 convert_bitcast_fusion.1
  1.3 0.7 convert_bitcast_fusion
  2.0 0.7 pad_bitcast_fusion
  2.7 0.7 pad_bitcast_fusion.2
  3.4 0.1 tile.17
  3.5 0.1 tile.19
  3.6 0.6 pad_maximum_fusion.meta_ref
  4.2 103.0 %window.1 = (bf16[32,2048]{1,0:T(8,128)(2,1)}, bf16[32,2048]{1,0:T(8,128)(2,1)}, f32[8,128]{1,0:T(8,128)}) custom-call(bf16[32,2048]{1,0:T(8,128)(2,1)} %tok_hbm.1, bf16[32,2048]{1,0:T(8,128)(2,1)} %cot_hbm.1, f32[2,2,8,128]{3,2,1,0:T(8,128)} %pad_maximum_fusion.meta_ref, bf16[7,32,704]{2,1,0:T(8,128)(2,1)} %bitcast.32, bf16[7,32,704]{2,1,0:T(8,128)(2,1)} %bitcast.33, ...), custom_call_target="tpu_custom_call" | custom-call | tf_op jit(solution)/shard_map/window/pallas_call | solution.py:348
  107.2 1.3 %slice_bitcast_fusion = f32[32,6]{0,1:T(8,128)} fusion(f32[8,128]{1,0:T(8,128)} %get-tuple-element.8), kind=kLoop, calls=%fused_computation.3 | loop fusion | bytes 1536 | tf_op jit(solution)/shard_map/transpose | solution.py:416
  108.5 1.6 %copy.16 = bf16[32,2048]{1,0:T(8,128)(2,1)} copy(bf16[32,2048]{1,0:T(8,128)(2,1)} %get-tuple-element.16) | data formatting | bytes 262144
  110.0 1.6 %copy.17 = bf16[32,2048]{1,0:T(8,128)(2,1)} copy(bf16[32,2048]{1,0:T(8,128)(2,1)} %get-tuple-element.17) | data formatting | bytes 262144
  (4 shorter events, 0.0 us)

commit v2 on v1

--- a/solution.py
+++ b/solution.py
@@ -43,10 +43,10 @@
 
 
 def kernel(
-    tok_hbm, cot_hbm, meta_ref, sg_hbm, su_hbm, wg_hbm, wu_hbm, wd_hbm,
+    tok_hbm, cot_hbm, routes_f, routes_b, factors_f, factors_b, sg_hbm, su_hbm, wg_hbm, wu_hbm, wd_hbm,
     mixed_hbm, grad_hbm, wgrad_ref,
     wg, wu, wd, sg, su, G, XS, X, OUT, OR, PS, R, SB, OB, MS, MR, SCS, SCR, SYS, SYR,
-    S, CH, CL, MT, acc_a, acc_b, co_g, co_u, co_s,
+    S, CH, MT, acc_a, acc_b, co_g, co_u, co_s,
     ag_s, ag_r, xd_s, xd_r, xr_s, xr_r, rs_s, rs_r, mt_s, mt_r, sc_s, sc_r, sy_s, sy_r, ld, own, outs,
 ):
     me = lax.axis_index("expert")
@@ -109,25 +109,30 @@
         pl.semaphore_signal(barrier, inc=1, device_id=at_x(p))
     loads = [
         pltpu.make_async_copy(a, b, ld.at[i])
-        for i, (a, b) in enumerate(((wg_hbm, wg), (wu_hbm, wu), (wd_hbm, wd), (sg_hbm, sg), (su_hbm, su)))
+        for i, (a, b) in enumerate(((sg_hbm, sg), (su_hbm, su), (wg_hbm, wg), (wu_hbm, wu), (wd_hbm, wd)))
     ]
+    for load in loads[:2]:
+        load.start()
     for m in range(2):
         for c in range(NC):
             own_rows(m, c).start()
-    for load in loads:
+    for load in loads[2:]:
         load.start()
 
     lane = iota((NY, 128), 1)
     named = (wrap(y + iota((NY, 128), 0), NY) * NX + wrap(x + lane // TOK, NX)).astype(F32)
     before = (iota((128, 128), 0) // TOK == iota((128, 128), 1) // TOK) & (iota((128, 128), 0) < iota((128, 128), 1))
     before = before.astype(F32).astype(BF16)
-    table = []
-    for m in range(2):
+    table, chosen = [], []
+    for routes, factors in ((routes_f, factors_f), (routes_b, factors_b)):
+        ids = jnp.concatenate([routes[...].astype(F32)] * NX, axis=1)
+        shares = jnp.concatenate([factors[...]] * NX, axis=1)
+        chosen.append(ids)
         has, weight = jnp.zeros((NY, 128), F32), jnp.zeros((NY, 128), F32)
         for k in range(TOPK):
-            hit = named == meta_ref[m, 0, k:k + 1, :]
+            hit = named == ids[k:k + 1, :]
             has = has + jnp.where(hit, 1.0, 0.0)
-            weight = weight + jnp.where(hit, meta_ref[m, 1, k:k + 1, :], 0.0)
+            weight = weight + jnp.where(hit, shares[k:k + 1, :], 0.0)
         slot = nn(has.astype(BF16), before)
         table += [jnp.where(has > 0, slot, -1.0), weight]
     for o in range(NY):
@@ -156,12 +161,13 @@
                     gather_hop(m, c, way, h - 1).wait_recv()
                     gather_hop(m, c, way, h).start()
 
-    start_own(0)
     for o in range(1, NY):
         meta_to(o).start()
-
-    loads[3].wait()
-    loads[4].wait()
+    start_own(0)
+    pass_on(0, 1)
+
+    loads[0].wait()
+    loads[1].wait()
     r, cj = iota((SLOTS, CAP * TOK), 0), iota((SLOTS, CAP * TOK), 1)
     source = wrap(y + r % NY, NY) * NX + wrap(x + r // PAD, NX)
     order = ((r % PAD) // NY == cj // 32) & (source == cj % 32)
@@ -175,10 +181,7 @@
     co_u[...] = act
     co_s[...] = act * u
 
-    pass_on(0, 1)
     pass_on(0, 2)
-    start_own(1)
-    pass_on(0, 3)
 
     for o in range(1, NY):
         meta_to(o).wait_recv()
@@ -194,24 +197,25 @@
         weights = jnp.broadcast_to(weights[None], (SLOTS // NY, NY, 128)).reshape(SLOTS, 128)
         hit = (slots == ((r128 % PAD) // NY).astype(F32)) & place
         match = jnp.where(hit, 1.0, 0.0).astype(BF16)
-        top, rest = halves(jnp.where(hit, weights, 0.0))
+        top = jnp.where(hit, weights, 0.0).astype(BF16)
         S[m] = jnp.where(block, nt(match, fold), 0.0).astype(BF16)
         CH[m] = jnp.where(back, nt(fold, top), 0.0).astype(BF16)
-        CL[m] = jnp.where(back, nt(fold, rest), 0.0).astype(BF16)
         if m == 1:
             MT[...] = match
 
-    def send_slots(m):
-        for c in range(NC):
-            own_rows(m, c).wait()
-            for way in (DOWN, UP):
-                gather_hop(m, c, way, hops(c, way) - 1).wait_recv()
-            rows = nn(S[m], G[m, c].reshape(NY * TOK, W)).astype(BF16).reshape(NX, PAD, W)
-            for p in range(1, NX):
-                XS[m, c, p - 1] = rows[p]
-            for p in (2, 1, 3):
-                to_expert(m, c, p).start()
-            X[m, c, 0] = rows[0]
+    pass_on(0, 3)
+    start_own(1)
+
+    def send_slots(m, c):
+        own_rows(m, c).wait()
+        for way in (DOWN, UP):
+            gather_hop(m, c, way, hops(c, way) - 1).wait_recv()
+        rows = nn(S[m], G[m, c].reshape(NY * TOK, W)).astype(BF16).reshape(NX, PAD, W)
+        for p in range(1, NX):
+            XS[m, c, p - 1] = rows[p]
+        for p in (2, 1, 3):
+            to_expert(m, c, p).start()
+        X[m, c, 0] = rows[0]
 
     def arrived(m, c):
         for p in range(1, NX):
@@ -226,37 +230,11 @@
             from_expert(m, c, q).start()
         OR[m, c, 0] = value[0]
 
-    send_slots(0)
-    pass_on(1, 1)
-    pass_on(1, 2)
-    pass_on(1, 3)
-    send_slots(1)
-
-    for load in loads[:3]:
-        load.wait()
-    for c in range(NC):
+    def forward(c):
         rows = arrived(0, c)
         g, v = nt(rows, wg[:, cols(c)]), nt(rows, wu[:, cols(c)])
         acc_a[...] = g if c == 0 else acc_a[...] + g
         acc_b[...] = v if c == 0 else acc_b[...] + v
-    g = acc_a[...]
-    hidden = (g / (1.0 + jnp.exp(-g)) * acc_b[...]).astype(BF16)
-    for c in range(NC):
-        give_back(0, c, nn(hidden, wd[:, cols(c)]))
-
-    for c in range(NC):
-        part = nt(arrived(1, c), wd[:, cols(c)])
-        acc_a[...] = part if c == 0 else acc_a[...] + part
-    gh = acc_a[...]
-    gg, gu = (gh * co_g[...]).astype(BF16), (gh * co_u[...]).astype(BF16)
-    top, rest = halves(gh * co_s[...])
-    for c in range(NC):
-        give_back(1, c, nn(gg, wg[:, cols(c)]) + nn(gu, wu[:, cols(c)]))
-    ones = jnp.ones((NY, ff), BF16)
-    score = nt(ones, top) + nt(ones, rest)
-    SCS[...] = score
-    for q in range(1, NX):
-        score_to(q).start()
 
     def send_sum(m, c, way, k):
         o = NY - k if way == DOWN else k
@@ -272,7 +250,7 @@
             for p in range(1, NX):
                 from_expert(m, c, NX - p).wait_recv()
             rows = OR[m, c].reshape(SLOTS, W)
-            PS[m, c] = (nn(CH[m], rows) + nn(CL[m], rows)).reshape(NY, TOK, W)
+            PS[m, c] = nn(CH[m], rows).reshape(NY, TOK, W)
         for way in (DOWN, UP):
             if hops(c, way) > s:
                 send_sum(m, c, way, hops(c, way) - s)
@@ -305,23 +283,67 @@
         for o in range(1, NY):
             score_back(o).wait_recv()
         rows = jnp.concatenate([SYR[o, 0:1, :] for o in range(NY)], axis=0)
-        for k in range(8):
-            v = jnp.sum(jnp.where(named == meta_ref[1, 0, k:k + 1, :], rows, 0.0), axis=0, keepdims=True)
+        for k in range(TOPK):
+            v = jnp.sum(jnp.where(named == chosen[1][k:k + 1, :], rows, 0.0), axis=0, keepdims=True)
             v = jnp.broadcast_to(v, (8, 128))
             v = v + pltpu.roll(v, 64, 1)
             v = v + pltpu.roll(v, 32, 1)
-            wgrad_ref[k:k + 1, :] = v[0:1, :]
+            wgrad_ref[k:k + 1, :] = v[0:1, :TOK]
+
+    def backward(c):
+        part = nt(arrived(1, c), wd[:, cols(c)])
+        acc_a[...] = part if c == 0 else acc_a[...] + part
+
+    def add_up(m, s):
+        for c in range(NC):
+            stage(m, c, s)
+
+    for c in range(NC):
+        send_slots(0, c)
+    pass_on(1, 1)
+    for load in loads[2:]:
+        load.wait()
+    forward(0)
+    pass_on(1, 2)
+    forward(1)
+    pass_on(1, 3)
+    forward(2)
+    forward(3)
+    g = acc_a[...]
+    hidden = (g / (1.0 + jnp.exp(-g)) * acc_b[...]).astype(BF16)
+    for c in range(NC):
+        give_back(0, c, nn(hidden, wd[:, cols(c)]))
+    for c in range(NC):
+        send_slots(1, c)
+    add_up(0, 0)
+    backward(0)
+    backward(1)
+    add_up(0, 1)
+    backward(2)
+    backward(3)
+    add_up(0, 2)
+    gh = acc_a[...]
+    gg, gu = (gh * co_g[...]).astype(BF16), (gh * co_u[...]).astype(BF16)
+    top, rest = halves(gh * co_s[...])
+    for c in range(NC):
+        give_back(1, c, nn(gg, wg[:, cols(c)]) + nn(gu, wu[:, cols(c)]))
+        if c == 1:
+            add_up(0, 3)
+    ones = jnp.ones((NY, ff), BF16)
+    score = nt(ones, top) + nt(ones, rest)
+    SCS[...] = score
+    for q in range(1, NX):
+        score_to(q).start()
+    add_up(1, 0)
+    add_up(0, 4)
+    scores_on()
+    add_up(1, 1)
+    add_up(1, 2)
+    scores_home()
+    add_up(1, 3)
+    add_up(1, 4)
 
     items = [(m, c) for m in range(2) for c in range(NC)]
-    for wave in range(len(items) + 4):
-        for s in range(4, -1, -1):
-            if 0 <= wave - s < len(items):
-                stage(*items[wave - s], s)
-        if wave == NC:
-            scores_on()
-        if wave == NC + 4:
-            scores_home()
-
     for m, c in items:
         for way in (DOWN, UP):
             for h in range(hops(c, way)):
@@ -339,7 +361,7 @@
         result(m, c).wait()
 
 
-def window(tokens, cotangent, meta, saved_gate, saved_up, w_gate, w_up, w_down):
+def window(tokens, cotangent, routes, routes_back, factors, factors_back, saved_gate, saved_up, w_gate, w_up, w_down):
     depth, ff = tokens.shape[1], w_down.shape[0]
     W = depth // NC
     whole = pl.BlockSpec(memory_space=pl.ANY)
@@ -351,9 +373,9 @@
         out_shape=(
             jax.ShapeDtypeStruct((TOK, depth), BF16),
             jax.ShapeDtypeStruct((TOK, depth), BF16),
-            jax.ShapeDtypeStruct((8, 128), F32),
+            jax.ShapeDtypeStruct((TOPK, TOK), F32),
         ),
-        in_specs=[whole, whole, vmem, whole, whole, whole, whole, whole],
+        in_specs=[whole, whole, vmem, vmem, vmem, vmem, whole, whole, whole, whole, whole],
         out_specs=(whole, whole, vmem),
         scratch_shapes=[
             pltpu.VMEM((ff, depth), BF16),
@@ -378,7 +400,6 @@
             pltpu.VMEM((NY, 8, 128), F32),
             pltpu.VMEM((2, SLOTS, SLOTS), BF16),
             pltpu.VMEM((2, SLOTS, SLOTS), BF16),
-            pltpu.VMEM((2, SLOTS, SLOTS), BF16),
             pltpu.VMEM((SLOTS, 128), BF16),
             pltpu.VMEM((SLOTS, ff), F32),
             pltpu.VMEM((SLOTS, ff), F32),
@@ -395,25 +416,27 @@
         compiler_params=pltpu.CompilerParams(
             collective_id=0, has_side_effects=True, vmem_limit_bytes=60 * 1024 * 1024
         ),
-    )(tokens, cotangent, meta, saved_gate, saved_up, w_gate, w_up, w_down)
-
-
-def lanes(routes, weights):
-    ids = jnp.pad(routes.T.astype(F32), ((0, 8 - TOPK), (0, 0)), constant_values=-1.0)
-    factors = jnp.pad(weights.T, ((0, 8 - TOPK), (0, 0)))
-    return jnp.tile(jnp.stack([ids, factors]), (1, 1, 128 // TOK))
+    )(tokens, cotangent, routes, routes_back, factors, factors_back, saved_gate, saved_up, w_gate, w_up, w_down)
+
+
+def hand_over(a_ref, b_ref, c_ref, a_out, b_out, c_out):
+    a_out[...] = a_ref[...]
+    b_out[...] = b_ref[...]
+    c_out[...] = c_ref[...]
 
 
 def body(
     tokens, routes, weights_fwd, cotangent, routes_back, weights_back, saved_gate, saved_up, w_gate, w_up, w_down
 ):
-    meta = jnp.stack([lanes(routes, weights_fwd), lanes(routes_back, weights_back)])
-    mixed, input_grad, wgrad = window(
-        tokens, cotangent, meta,
+    parts = window(
+        tokens, cotangent, routes.T, routes_back.T, weights_fwd.T, weights_back.T,
         saved_gate[0, :, 0].transpose(1, 0, 2), saved_up[0, :, 0].transpose(1, 0, 2),
         w_gate[0].T, w_up[0].T, w_down[0],
     )
-    return mixed, input_grad, wgrad[:TOPK, :TOK].T
+    mixed, input_grad, wgrad = pl.pallas_call(
+        hand_over, name="hand_over", out_shape=tuple(jax.ShapeDtypeStruct(v.shape, v.dtype) for v in parts)
+    )(*parts)
+    return mixed, input_grad, wgrad.T
 
 
 def solution(mesh):

time: 112 us -> 94.9 us (0.85)
  the two profiles are of different devices: /device:TPU:16 before, /device:TPU:2 now
where the time goes in v2:
time: 94.9 us; the launch traced here: 94.7 us
  Pallas kernels  94 us (99%)
    pallas_call x1, Pallas kernels, window(): pl.pallas_call(kernel, name='window', out_shape=(jax.ShapeDtypeStruct((TO...  92.3 us

profile of v2, /device:TPU:2, one launch (start us, length us, event | category | flops | bytes accessed | tf_op | source)
XLA Modules:
  0.0 94.7 jit_solution(8920204336528544457)
XLA Ops:
  0.6 92.3 %window.1 = (bf16[32,2048]{1,0:T(8,128)(2,1)}, bf16[32,2048]{1,0:T(8,128)(2,1)}, f32[6,32]{1,0:T(8,128)}) custom-call(bf16[32,2048]{1,0:T(8,128)(2,1)} %tok_hbm.1, bf16[32,2048]{1,0:T(8,128)(2,1)} %cot_hbm.1, s32[6,32]{1,0:T(8,128)} %bitcast.23, s32[6,32]{1,0:T(8,128)} %bitcast.24, f32[6,32]{1,0:T(8,128)} %bitcast.25, f32[6,32]{1,0:T(8,128)} %bitcast.26, ...), custom_call_target="tpu_custom_call" | custom-call | tf_op jit(solution)/shard_map/window/pallas_call | solution.py:370
  93.0 1.7 %hand_over.1 = (bf16[32,2048]{1,0:T(8,128)(2,1)}, bf16[32,2048]{1,0:T(8,128)(2,1)}, f32[6,32]{1,0:T(8,128)}) custom-call(bf16[32,2048]{1,0:T(8,128)(2,1)} %get-tuple-element.9.a_ref, bf16[32,2048]{1,0:T(8,128)(2,1)} %get-tuple-element.10.b_ref, f32[6,32]{1,0:T(8,128)} %get-tuple-element.11.c_ref), custom_call_target="tpu_custom_call" | custom-call | tf_op jit(solution)/shard_map/hand_over/pallas_call | solution.py:436

commit v3 on v2

--- a/solution.py
+++ b/solution.py
@@ -166,21 +166,6 @@
     start_own(0)
     pass_on(0, 1)
 
-    loads[0].wait()
-    loads[1].wait()
-    r, cj = iota((SLOTS, CAP * TOK), 0), iota((SLOTS, CAP * TOK), 1)
-    source = wrap(y + r % NY, NY) * NX + wrap(x + r // PAD, NX)
-    order = ((r % PAD) // NY == cj // 32) & (source == cj % 32)
-    order = order.astype(F32).astype(BF16)
-    ff = wd_hbm.shape[0]
-    a = nn(order, sg[...].reshape(CAP * 32, ff))
-    u = nn(order, su[...].reshape(CAP * 32, ff))
-    sig = 1.0 / (1.0 + jnp.exp(-a))
-    act = a * sig
-    co_g[...] = u * sig * (1.0 + a * (1.0 - sig))
-    co_u[...] = act
-    co_s[...] = act * u
-
     pass_on(0, 2)
 
     for o in range(1, NY):
@@ -190,7 +175,8 @@
     fold = (r128 % TOK == l128 % TOK).astype(F32).astype(BF16)
     block = iota((SLOTS, SLOTS), 0) % NY == iota((SLOTS, SLOTS), 1) // TOK
     back = iota((SLOTS, SLOTS), 1) % NY == iota((SLOTS, SLOTS), 0) // TOK
-    for m in range(2):
+
+    def tables(m):
         slots = jnp.concatenate([MR[o, 2 * m:2 * m + 1, :] for o in range(NY)], axis=0)
         weights = jnp.concatenate([MR[o, 2 * m + 1:2 * m + 2, :] for o in range(NY)], axis=0)
         slots = jnp.broadcast_to(slots[None], (SLOTS // NY, NY, 128)).reshape(SLOTS, 128)
@@ -203,6 +189,7 @@
         if m == 1:
             MT[...] = match
 
+    tables(0)
     pass_on(0, 3)
     start_own(1)
 
@@ -301,12 +288,28 @@
     for c in range(NC):
         send_slots(0, c)
     pass_on(1, 1)
+    loads[0].wait()
+    loads[1].wait()
+    r, cj = iota((SLOTS, CAP * TOK), 0), iota((SLOTS, CAP * TOK), 1)
+    source = wrap(y + r % NY, NY) * NX + wrap(x + r // PAD, NX)
+    order = ((r % PAD) // NY == cj // 32) & (source == cj % 32)
+    order = order.astype(F32).astype(BF16)
+    ff = wd_hbm.shape[0]
+    a = nn(order, sg[...].reshape(CAP * 32, ff))
+    u = nn(order, su[...].reshape(CAP * 32, ff))
+    sig = 1.0 / (1.0 + jnp.exp(-a))
+    act = a * sig
+    co_g[...] = u * sig * (1.0 + a * (1.0 - sig))
+    co_u[...] = act
+    co_s[...] = act * u
+
     for load in loads[2:]:
         load.wait()
+    pass_on(1, 2)
+    tables(1)
     forward(0)
-    pass_on(1, 2)
+    pass_on(1, 3)
     forward(1)
-    pass_on(1, 3)
     forward(2)
     forward(3)
     g = acc_a[...]

time: 94.9 us -> 93.1 us (0.981)
  Pallas kernels: 94 us -> 92.3 us
    pallas_call x1, Pallas kernels: 92.3 us -> 90.6 us  [window(): pl.pallas_call(kernel, name='window', out_shape=(jax.ShapeDtypeStruct((TO...]
where the time goes in v3:
time: 93.1 us; the launch traced here: 92.9 us
  Pallas kernels  92.3 us (99%)
    pallas_call x1, Pallas kernels, window(): pl.pallas_call(kernel, name='window', out_shape=(jax.ShapeDtypeStruct((TO...  90.6 us

profile of v3, /device:TPU:2, one launch (start us, length us, event | category | flops | bytes accessed | tf_op | source)
XLA Modules:
  0.0 92.9 jit_solution(13153903026629230069)
XLA Ops:
  0.6 90.6 %window.1 = (bf16[32,2048]{1,0:T(8,128)(2,1)}, bf16[32,2048]{1,0:T(8,128)(2,1)}, f32[6,32]{1,0:T(8,128)}) custom-call(bf16[32,2048]{1,0:T(8,128)(2,1)} %tok_hbm.1, bf16[32,2048]{1,0:T(8,128)(2,1)} %cot_hbm.1, s32[6,32]{1,0:T(8,128)} %bitcast.23, s32[6,32]{1,0:T(8,128)} %bitcast.24, f32[6,32]{1,0:T(8,128)} %bitcast.25, f32[6,32]{1,0:T(8,128)} %bitcast.26, ...), custom_call_target="tpu_custom_call" | custom-call | tf_op jit(solution)/shard_map/window/pallas_call | solution.py:373
  91.2 1.7 %hand_over.1 = (bf16[32,2048]{1,0:T(8,128)(2,1)}, bf16[32,2048]{1,0:T(8,128)(2,1)}, f32[6,32]{1,0:T(8,128)}) custom-call(bf16[32,2048]{1,0:T(8,128)(2,1)} %get-tuple-element.9.a_ref, bf16[32,2048]{1,0:T(8,128)(2,1)} %get-tuple-element.10.b_ref, f32[6,32]{1,0:T(8,128)} %get-tuple-element.11.c_ref), custom_call_target="tpu_custom_call" | custom-call | tf_op jit(solution)/shard_map/hand_over/pallas_call | solution.py:439
